TPU v7x, 128 devices: a whole 4x4x4 slice. The times are simulated.
128 devices in a mesh: section: 8 (over y, core), tp: 16 (over x, z).
Axes of the slice: x: 4, y: 4, z: 4, core: 2. Of those that a mesh axis runs over, the one named last changes fastest.
Arguments:
- stream_in: bfloat16 [512, 8192], P(None, 'tp')
- layer_delta: bfloat16 [8, 512, 8192], P('section', None, 'tp')
- norm_gain: float32 [8192], P('tp'), may hold values from 0.25 to 1.75
- out_embed: bfloat16 [8192, 16384], P(None, 'tp')
- exit_blocks: int32 [8, 4], P('section'), may hold values from 0 to 3
- exit_counts: int32 [8], P('section'), may hold values from 1 to 4, 16 in all
- targets: int32 [512], replicated, may hold values from 0 to 16383
Outputs:
- exit_loss: float32 [8, 4, 128], P('section')
Inputs may be any that keep to these rules, and one draw needn't show every extreme that they name: `exit_counts`: each section scores at least one block, the counts of all sections sum to 2 times the number of sections, and some section scores exactly 4. `exit_blocks`: block numbers of the micro-batch's 128-row blocks; only a section's first exit_counts entries are used.
All inputs are finite; a program needn't handle non-finite values.
Results may differ from a plain program's by a relative error of at most 0.02.
Values may be sent and summed in bfloat16 or wider, within the bound.
A program may use at most 128 MiB of HBM per device.

v0:
```python
import jax
import jax.numpy as jnp
from jax import lax
from jax.sharding import PartitionSpec as P

BLK = 128
MAXB = 4
EPS = 1e-05


def prefix(shard, axis, join, neutral):
    place = lax.axis_index(axis)
    gathered = lax.all_gather(shard.astype(jnp.bfloat16), axis)
    state = jnp.zeros_like(shard) + jnp.asarray(neutral, shard.dtype)

    def one(lap, state):
        return join(state, lax.dynamic_index_in_dim(gathered, lap, 0, False).astype(shard.dtype))

    return lax.fori_loop(0, place, one, state)


def from_root(shard, axis, root):
    mine = lax.axis_index(axis) == root
    return lax.psum(jnp.where(mine, shard, jnp.zeros_like(shard)), axis)


def add_terms(first, second):
    return first + second


def row_losses(exit_rows, teach_rows, target_rows, norm_gain, out_embed):
    width = out_embed.shape[0]
    squares = lax.psum(
        (jnp.sum(exit_rows * exit_rows, axis=1), jnp.sum(teach_rows * teach_rows, axis=1)), "tp"
    )
    normed_exit = (
        exit_rows * lax.rsqrt(squares[0] / width + EPS)[:, None] * norm_gain[None, :]
    ).astype(jnp.bfloat16)
    normed_teach = (
        teach_rows * lax.rsqrt(squares[1] / width + EPS)[:, None] * norm_gain[None, :]
    ).astype(jnp.bfloat16)
    vocab_part = out_embed.shape[1]
    logit_exit = jnp.dot(
        lax.all_gather(normed_exit, "tp", axis=1, tiled=True),
        out_embed,
        preferred_element_type=jnp.float32,
    )
    logit_teach = jnp.dot(
        lax.all_gather(normed_teach, "tp", axis=1, tiled=True),
        out_embed,
        preferred_element_type=jnp.float32,
    )
    first_column = lax.axis_index("tp") * vocab_part
    columns = jnp.arange(vocab_part, dtype=jnp.int32)
    hit = (target_rows - first_column)[:, None] == columns[None, :]
    target_part = jnp.sum(jnp.where(hit, logit_exit, 0.0), axis=1)
    peak_exit, peak_teach = lax.pmax(
        (jnp.max(logit_exit, axis=1), jnp.max(logit_teach, axis=1)), "tp"
    )
    weight_teach = jnp.exp(logit_teach - peak_teach[:, None])
    total_exit, total_teach, cross, picked = lax.psum(
        (
            jnp.sum(jnp.exp(logit_exit - peak_exit[:, None]), axis=1),
            jnp.sum(weight_teach, axis=1),
            jnp.sum(weight_teach * (logit_teach - logit_exit), axis=1),
            target_part,
        ),
        "tp",
    )
    log_exit = jnp.log(total_exit) + peak_exit
    log_teach = jnp.log(total_teach) + peak_teach
    return 2.0 * log_exit - picked + cross / total_teach - log_teach


def body(stream_in, layer_delta, norm_gain, out_embed, exit_blocks, exit_counts, targets):
    stream = stream_in.astype(jnp.float32)
    mine_delta = layer_delta[0].astype(jnp.float32)
    before = prefix(mine_delta, "section", add_terms, jnp.zeros_like(mine_delta))
    exit_all = stream + before + mine_delta
    final_all = from_root(
        exit_all.astype(jnp.bfloat16), "section", lax.axis_size("section") - 1
    ).astype(exit_all.dtype)
    starts = [exit_blocks[0, slot_index] * BLK for slot_index in range(MAXB)]
    exit_rows = jnp.concatenate(
        [lax.dynamic_slice_in_dim(exit_all, start, BLK, 0) for start in starts], axis=0
    )
    teach_rows = jnp.concatenate(
        [lax.dynamic_slice_in_dim(final_all, start, BLK, 0) for start in starts], axis=0
    )
    target_rows = jnp.concatenate(
        [lax.dynamic_slice_in_dim(targets, start, BLK, 0) for start in starts], axis=0
    )
    losses = row_losses(exit_rows, teach_rows, target_rows, norm_gain, out_embed).reshape(MAXB, BLK)
    keep = jnp.arange(MAXB, dtype=jnp.int32) < exit_counts[0]
    return jnp.where(keep[:, None], losses, 0.0)[None]


def solution(mesh):
    placed = (
        P(None, "tp"),
        P("section", None, "tp"),
        P("tp"),
        P(None, "tp"),
        P("section", None),
        P("section"),
        P(),
    )
    return jax.shard_map(
        body, mesh=mesh, in_specs=placed, out_specs=P("section", None, None), check_vma=False
    )
```

profile of v0, /device:TPU:0, one launch (start us, length us, event | category | flops | bytes accessed | tf_op | source)
XLA Modules:
  0.0 407.7 jit_solution(8671719075948042999)
XLA Ops:
  6.5 0.7 all-gather.4.cloned.1.call-update
  7.3 0.0 all-reduce.5.cloned.1.call-start
  7.3 36.3 %all-gather.4.cloned.1.call-done = bf16[8,512,512]{2,1,0:T(8,128)(2,1)} async-done(((bf16[1,512,512]{2,1,0:T(8,128)(2,1)}), bf16[8,512,512]{2,1,0:T(8,128)(2,1)}) %all-gather.4.cloned.1.call-update) | async-done | bytes 4194320 | tf_op jit(solution)/shard_map/all_gather | solution.py:13
  43.6 0.1 broadcast_in_dim.21
  43.8 0.0 copy-start
  43.8 1.0 copy-done
  44.8 0.3 copy-done.1
  45.1 1.1 convert_select_fusion
  46.2 0.0 all-reduce.5.cloned.1.call-update
  46.2 0.0 all-gather.8.cloned.1.call-start
  46.2 0.7 fusion.3
  49.5 0.1 constant_dynamic-slice_fusion.7
  49.6 0.1 multiply_reduce_fusion.2
  49.8 0.0 copy-start.4
  49.8 64.8 %all-reduce.5.cloned.1.call-done = bf16[512,512]{1,0:T(8,128)(2,1)} async-done(((bf16[512,512]{1,0:T(8,128)(2,1)}), bf16[512,512]{1,0:T(8,128)(2,1)}) %all-reduce.5.cloned.1.call-update) | async-done | bytes 524304 | tf_op jit(solution)/shard_map/psum | solution.py:24
  114.6 1.2 convert_element_type.33
  115.8 0.1 constant_dynamic-slice_fusion.3
  115.9 0.2 multiply_reduce_fusion.1
  116.0 40.5 %all-reduce.1 = (f32[512]{0:T(512)S(1)}, f32[512]{0:T(512)S(1)}) all-reduce(f32[512]{0:T(512)S(1)} %multiply_reduce_fusion.1, f32[512]{0:T(512)S(1)} %multiply_reduce_fusion.2), channel_id=1, replica_groups=mesh['section'=8,'tp'=16] {'tp'}, use_global_device_ids=true, to_apply=%region_12.13 | all-reduce | flops 1024 | bytes 8192 | tf_op jit(solution)/shard_map/psum | solution.py:33
  156.6 1.3 multiply_convert_fusion.1
  157.8 0.0 all-gather.8.cloned.1.call-update
  157.9 0.0 all-gather.6.cloned.1.call-start
  157.9 0.5 all-gather.6.cloned.1.call-update
  159.1 0.1 fusion.2
  159.2 69.9 %all-gather.8.cloned.1.call-done = bf16[512,8192]{1,0:T(8,128)(2,1)} async-done(((bf16[512,512]{1,0:T(8,128)(2,1)}), bf16[512,8192]{1,0:T(8,128)(2,1)}) %all-gather.8.cloned.1.call-update) | async-done | bytes 8388624 | tf_op jit(solution)/shard_map/all_gather | solution.py:49
  229.1 14.8 %fusion.4 = (f32[512]{0:T(512)S(1)}, f32[512,1024]{1,0:T(8,128)S(1)}) fusion(bf16[512,8192]{1,0:T(8,128)(2,1)} %all-gather.8.cloned.1.call-done, bf16[8192,1024]{1,0:T(8,128)(2,1)} %param.12), kind=kOutput, calls=%fused_computation.31 | convolution fusion | flops 8590458880 | bytes 27265024 | tf_op jit(solution)/shard_map/dot_general | solution.py:48
  243.9 63.8 %all-gather.6.cloned.1.call-done = bf16[512,8192]{1,0:T(8,128)(2,1)} async-done(((bf16[512,512]{1,0:T(8,128)(2,1)}), bf16[512,8192]{1,0:T(8,128)(2,1)}) %all-gather.6.cloned.1.call-update) | async-done | bytes 8388624 | tf_op jit(solution)/shard_map/all_gather | solution.py:44
  307.7 16.0 %fusion.1 = (f32[512]{0:T(512)S(1)}, f32[512]{0:T(512)S(1)}, f32[512,1024]{1,0:T(8,128)}) fusion(s32[512]{0:T(512)S(1)} %add_subtract_fusion, bf16[512,8192]{1,0:T(8,128)(2,1)} %all-gather.6.cloned.1.call-done, bf16[8192,1024]{1,0:T(8,128)(2,1)} %param.12), kind=kOutput, calls=%fused_computation.28 | convolution fusion | flops 8592031744 | bytes 27269120 | tf_op jit(solution)/shard_map/dot_general | solution.py:43
  323.7 38.1 %all-reduce.2 = (f32[512]{0:T(512)S(1)}, f32[512]{0:T(512)S(1)}) all-reduce(f32[512]{0:T(512)S(1)} %get-tuple-element.70, f32[512]{0:T(512)S(1)} %get-tuple-element.32), channel_id=1, replica_groups=mesh['section'=8,'tp'=16] {'tp'}, use_global_device_ids=true, to_apply=%region_14.15 | all-reduce | flops 1024 | bytes 8192 | tf_op jit(solution)/shard_map/pmax | solution.py:57
  361.8 2.7 multiply_reduce_fusion
  364.5 35.9 %all-reduce = (f32[512]{0:T(512)S(1)}, f32[512]{0:T(512)S(1)}, f32[512]{0:T(512)S(1)}, f32[512]{0:T(512)S(1)}) all-reduce(f32[512]{0:T(512)S(1)} %get-tuple-element.30, f32[512]{0:T(512)S(1)} %get-tuple-element.29, f32[512]{0:T(512)S(1)} %get-tuple-element.33, f32[512]{0:T(512)S(1)} %get-tuple-element.31), channel_id=1, replica_groups=mesh['section'=8,'tp'=16] {'tp'}, use_global_device_ids=true, to_apply=%region_18.19 | all-reduce | flops 2048 | bytes 16384 | tf_op jit(solution)/shard_map/psum | solution.py:61
  400.5 0.7 bitcast_select_fusion
  (11 shorter events, 0.1 us)
Async XLA Ops:
  6.5 37.1 %all-gather.4.cloned.1.call-start = ((), (), s32[]{:S(2)}) async-start(), calls=%async_computation | async-start | bytes 4718592 | tf_op jit(solution)/shard_map/all_gather | solution.py:13
  7.3 107.4 %all-reduce.5.cloned.1.call-start = ((), (), s32[]{:S(2)}) async-start(), calls=%async_computation.2 | async-start | bytes 1048576 | tf_op jit(solution)/shard_map/psum | solution.py:24
  43.8 1.0 copy-start
  43.8 1.3 copy-start.1
  45.1 1.1 copy-start.2
  46.2 182.9 %all-gather.8.cloned.1.call-start = ((), (), s32[]{:S(2)}) async-start(), calls=%async_computation.3 | async-start | bytes 8912896 | tf_op jit(solution)/shard_map/all_gather | solution.py:49
  49.8 106.8 %copy-start.4 = (f32[512]{0:T(512)S(1)}, f32[512]{0:T(512)}, u32[]{:S(2)}) copy-start(f32[512]{0:T(512)} %param.11) | copy-start | bytes 6148
  156.6 2.5 copy-start.3
  157.9 149.8 %all-gather.6.cloned.1.call-start = ((), (), s32[]{:S(2)}) async-start(), calls=%async_computation.1 | async-start | bytes 8912896 | tf_op jit(solution)/shard_map/all_gather | solution.py:44
Sparse Core Ops, SparseCore 0:
  9.0 34.5 all-gather.3
  46.3 68.2 all-reduce.4
  158.0 71.0 all-gather.7
  231.1 76.6 all-gather.5
where the time goes:
time: 408 us
  waiting for transfers between devices  236 us (58%)
  blocking collectives  115 us (28%)
  matrix products  30.8 us (8%)
  between operations  16.5 us (4%)
  other arithmetic  7.16 us (2%)
    all_gather x1, waiting for transfers between devices, row_losses(): lax.all_gather(normed_teach, 'tp', axis=1, tiled=True)  69.9 us
    psum x1, waiting for transfers between devices, from_root(): return lax.psum(jnp.where(mine, shard, jnp.zeros_like(shard)), axis)  64.8 us
    all_gather x1, waiting for transfers between devices, row_losses(): lax.all_gather(normed_exit, 'tp', axis=1, tiled=True)  63.8 us
    psum x1, blocking collectives, row_losses(): lax.psum((jnp.sum(exit_rows * exit_rows, axis=1), jnp.sum(teach_rows * te...  40.5 us
    pmax x1, blocking collectives, row_losses(): lax.pmax((jnp.max(logit_exit, axis=1), jnp.max(logit_teach, axis=1)), 'tp')  38.1 us
    all_gather x1, waiting for transfers between devices, prefix(): gathered = lax.all_gather(shard.astype(jnp.bfloat16), axis)  36.3 us
    psum x1, blocking collectives, row_losses(): lax.psum((jnp.sum(jnp.exp(logit_exit - peak_exit[:, None]), axis=1), jnp....  35.9 us
    dot_general x1, matrix products, row_losses(): jnp.dot(lax.all_gather(normed_exit, 'tp', axis=1, tiled=True), out_embed,...  16 us
  transfers between devices with their start and end apart: 4, of which 4 were waited for; matrix products, arithmetic and copies ran while one was open for 4% of the time, Pallas kernels for 0%

commit v1 on v0

--- a/solution.py
+++ b/solution.py
@@ -6,6 +6,13 @@
 BLK = 128
 MAXB = 4
 EPS = 1e-05
+
+
+def swapped_in(x, axis, d):
+    count = lax.axis_size(axis)
+    blocks = jnp.stack([x for _ in range(count)])
+    blocks = lax.all_to_all(blocks, axis, split_axis=0, concat_axis=0)
+    return jnp.concatenate(blocks, axis=d)
 
 
 def prefix(shard, axis, join, neutral):
@@ -41,9 +48,7 @@
     ).astype(jnp.bfloat16)
     vocab_part = out_embed.shape[1]
     logit_exit = jnp.dot(
-        lax.all_gather(normed_exit, "tp", axis=1, tiled=True),
-        out_embed,
-        preferred_element_type=jnp.float32,
+        swapped_in(normed_exit, "tp", 1), out_embed, preferred_element_type=jnp.float32
     )
     logit_teach = jnp.dot(
         lax.all_gather(normed_teach, "tp", axis=1, tiled=True),

time: 408 us -> 422 us (1.034)
  starting transfers between devices: 0.12 us -> 5.01 us
  local copies, waits for them, and re-layouts: 2.36 us -> 6.6 us
    all_to_all x0 -> x1, waiting for transfers between devices: none -> 103 us  [swapped_in(): blocks = lax.all_to_all(blocks, axis, split_axis=0, concat_axis=0)]
    all_gather x1 -> x0, waiting for transfers between devices: 63.8 us -> none  [row_losses(): lax.all_gather(normed_exit, 'tp', axis=1, tiled=True)]
    all_gather x1, waiting for transfers between devices: 69.9 us -> 34.8 us  [row_losses(): lax.all_gather(normed_teach, 'tp', axis=1, tiled=True)]
    all_to_all x0 -> x1, starting transfers between devices: none -> 4.93 us  [swapped_in(): blocks = lax.all_to_all(blocks, axis, split_axis=0, concat_axis=0)]
  transfers between devices with their start and end apart: 4 -> 4, of which waited for: 4 -> 4; matrix products, arithmetic and copies ran while one was open for 4% -> 5% of each run, Pallas kernels for 0% -> 0%
where the time goes in v1:
time: 422 us; the launch traced here: 421 us
  waiting for transfers between devices  240 us (57%)
  blocking collectives  115 us (27%)
  matrix products  31.5 us (7%)
  between operations  16.5 us (4%)
  other arithmetic  6.98 us (2%)
  local copies, waits for them, and re-layouts  6.6 us (2%)
  starting transfers between devices  5.01 us (1%)
    all_to_all x1, waiting for transfers between devices, swapped_in(): blocks = lax.all_to_all(blocks, axis, split_axis=0, concat_axis=0)  103 us
    psum x1, waiting for transfers between devices, from_root(): return lax.psum(jnp.where(mine, shard, jnp.zeros_like(shard)), axis)  64.9 us
    psum x1, blocking collectives, row_losses(): lax.psum((jnp.sum(exit_rows * exit_rows, axis=1), jnp.sum(teach_rows * te...  40.5 us
    pmax x1, blocking collectives, row_losses(): lax.pmax((jnp.max(logit_exit, axis=1), jnp.max(logit_teach, axis=1)), 'tp')  38.1 us
    all_gather x1, waiting for transfers between devices, prefix(): gathered = lax.all_gather(shard.astype(jnp.bfloat16), axis)  36.3 us
    psum x1, blocking collectives, row_losses(): lax.psum((jnp.sum(jnp.exp(logit_exit - peak_exit[:, None]), axis=1), jnp....  35.9 us
    all_gather x1, waiting for transfers between devices, row_losses(): lax.all_gather(normed_teach, 'tp', axis=1, tiled=True)  34.8 us
    dot_general x1, matrix products, row_losses(): jnp.dot(lax.all_gather(normed_teach, 'tp', axis=1, tiled=True), out_embed...  16 us
  transfers between devices with their start and end apart: 4, of which 4 were waited for; matrix products, arithmetic and copies ran while one was open for 5% of the time, Pallas kernels for 0%

profile of v1, /device:TPU:0, one launch (start us, length us, event | category | flops | bytes accessed | tf_op | source)
XLA Modules:
  0.0 421.4 jit_solution(7865122768724224138)
XLA Ops:
  6.5 0.7 all-gather.3.cloned.1.call-update
  7.3 0.0 all-reduce.5.cloned.1.call-start
  7.3 36.3 %all-gather.3.cloned.1.call-done = bf16[8,512,512]{2,1,0:T(8,128)(2,1)} async-done(((bf16[1,512,512]{2,1,0:T(8,128)(2,1)}), bf16[8,512,512]{2,1,0:T(8,128)(2,1)}) %all-gather.3.cloned.1.call-update) | async-done | bytes 4194320 | tf_op jit(solution)/shard_map/all_gather | solution.py:20
  43.6 0.1 broadcast_in_dim.21
  43.8 0.0 copy-start
  43.8 1.0 copy-done
  44.8 0.3 copy-done.1
  45.1 1.1 convert_select_fusion
  46.2 0.0 all-reduce.5.cloned.1.call-update
  46.2 0.0 all-gather.5.cloned.1.call-start
  46.2 0.7 fusion.3
  49.5 0.1 constant_dynamic-slice_fusion.7
  49.6 0.1 multiply_reduce_fusion.2
  49.8 64.9 %all-reduce.5.cloned.1.call-done = bf16[512,512]{1,0:T(8,128)(2,1)} async-done(((bf16[512,512]{1,0:T(8,128)(2,1)}), bf16[512,512]{1,0:T(8,128)(2,1)}) %all-reduce.5.cloned.1.call-update) | async-done | bytes 524304 | tf_op jit(solution)/shard_map/psum | solution.py:31
  114.7 1.2 convert_element_type.35
  115.9 0.1 constant_dynamic-slice_fusion.3
  116.0 0.2 multiply_reduce_fusion.1
  116.1 40.5 %all-reduce.1 = (f32[512]{0:T(512)S(1)}, f32[512]{0:T(512)S(1)}) all-reduce(f32[512]{0:T(512)S(1)} %multiply_reduce_fusion.1, f32[512]{0:T(512)S(1)} %multiply_reduce_fusion.2), channel_id=1, replica_groups=mesh['section'=8,'tp'=16] {'tp'}, use_global_device_ids=true, to_apply=%region_12.13 | all-reduce | flops 1024 | bytes 8192 | tf_op jit(solution)/shard_map/psum | solution.py:40
  156.7 1.1 multiply_convert_fusion.1
  157.7 0.0 all-gather.5.cloned.1.call-update
  157.8 0.2 copy.9
  158.0 4.0 stack.2
  162.0 4.9 %all-to-all-start = ((bf16[16,512,512]{1,2,0:T(8,128)(2,1)}), bf16[16,512,512]{1,2,0:T(8,128)(2,1)}, u32[]{:S(2)}, u32[]{:S(2)}) async-start(bf16[16,512,512]{1,2,0:T(8,128)(2,1)} %stack.2), calls=%async_computation | async-start | bytes 16777216 | tf_op jit(solution)/shard_map/all_to_all | solution.py:14
  167.6 0.1 fusion.2
  167.7 103.4 %all-to-all-done = bf16[16,512,512]{1,2,0:T(8,128)(2,1)} async-done(((bf16[16,512,512]{1,2,0:T(8,128)(2,1)}), bf16[16,512,512]{1,2,0:T(8,128)(2,1)}, u32[]{:S(2)}, u32[]{:S(2)}) %all-to-all-start) | async-done | bytes 8388640 | tf_op jit(solution)/shard_map/all_to_all | solution.py:14
  271.1 15.6 %fusion.1 = (f32[512]{0:T(512)S(1)}, f32[512]{0:T(512)S(1)}, f32[512,1024]{1,0:T(8,128)S(1)}) fusion(s32[512]{0:T(512)S(1)} %add_subtract_fusion, bf16[512,8192]{0,1:T(8,128)(2,1)} %bitcast.8, bf16[8192,1024]{1,0:T(8,128)(2,1)} %param.12), kind=kOutput, calls=%fused_computation.28 | convolution fusion | flops 8592031744 | bytes 27269120 | tf_op jit(solution)/shard_map/dot_general | solution.py:50
  286.7 34.8 %all-gather.5.cloned.1.call-done = bf16[512,8192]{1,0:T(8,128)(2,1)} async-done(((bf16[512,512]{1,0:T(8,128)(2,1)}), bf16[512,8192]{1,0:T(8,128)(2,1)}) %all-gather.5.cloned.1.call-update) | async-done | bytes 8388624 | tf_op jit(solution)/shard_map/all_gather | solution.py:54
  321.5 16.0 %fusion.4 = (f32[512]{0:T(512)S(1)}, f32[512,1024]{1,0:T(8,128)}) fusion(bf16[512,8192]{1,0:T(8,128)(2,1)} %all-gather.5.cloned.1.call-done, bf16[8192,1024]{1,0:T(8,128)(2,1)} %param.12), kind=kOutput, calls=%fused_computation.31 | convolution fusion | flops 8590458880 | bytes 27265024 | tf_op jit(solution)/shard_map/dot_general | solution.py:53
  337.5 38.1 %all-reduce.2 = (f32[512]{0:T(512)S(1)}, f32[512]{0:T(512)S(1)}) all-reduce(f32[512]{0:T(512)S(1)} %get-tuple-element.70, f32[512]{0:T(512)S(1)} %get-tuple-element.32), channel_id=1, replica_groups=mesh['section'=8,'tp'=16] {'tp'}, use_global_device_ids=true, to_apply=%region_14.15 | all-reduce | flops 1024 | bytes 8192 | tf_op jit(solution)/shard_map/pmax | solution.py:62
  375.6 2.7 multiply_reduce_fusion
  378.3 35.9 %all-reduce = (f32[512]{0:T(512)S(1)}, f32[512]{0:T(512)S(1)}, f32[512]{0:T(512)S(1)}, f32[512]{0:T(512)S(1)}) all-reduce(f32[512]{0:T(512)S(1)} %get-tuple-element.30, f32[512]{0:T(512)S(1)} %get-tuple-element.29, f32[512]{0:T(512)S(1)} %get-tuple-element.33, f32[512]{0:T(512)S(1)} %get-tuple-element.31), channel_id=1, replica_groups=mesh['section'=8,'tp'=16] {'tp'}, use_global_device_ids=true, to_apply=%region_18.19 | all-reduce | flops 2048 | bytes 16384 | tf_op jit(solution)/shard_map/psum | solution.py:66
  414.3 0.7 bitcast_select_fusion
  (12 shorter events, 0.1 us)
Async XLA Ops:
  6.5 37.1 %all-gather.3.cloned.1.call-start = ((), (), s32[]{:S(2)}) async-start(), calls=%async_computation.1 | async-start | bytes 4718592 | tf_op jit(solution)/shard_map/all_gather | solution.py:20
  7.3 107.4 %all-reduce.5.cloned.1.call-start = ((), (), s32[]{:S(2)}) async-start(), calls=%async_computation.2 | async-start | bytes 1048576 | tf_op jit(solution)/shard_map/psum | solution.py:31
  43.8 1.0 copy-start
  43.8 1.3 copy-start.1
  43.8 2.4 copy-start.2
  46.2 110.5 %copy-start.4 = (f32[512]{0:T(512)S(1)}, f32[512]{0:T(512)}, u32[]{:S(2)}) copy-start(f32[512]{0:T(512)} %param.11) | copy-start | bytes 6148
  46.2 275.3 %all-gather.5.cloned.1.call-start = ((), (), s32[]{:S(2)}) async-start(), calls=%async_computation.3 | async-start | bytes 8912896 | tf_op jit(solution)/shard_map/all_gather | solution.py:54
  162.0 5.6 %copy-start.3 = (s32[512]{0:T(512)S(1)}, s32[512]{0:T(512)}, u32[]{:S(2)}) copy-start(s32[512]{0:T(512)} %param.15) | copy-start | bytes 6148
  162.0 109.1 %all-to-all-start = ((bf16[16,512,512]{1,2,0:T(8,128)(2,1)}), bf16[16,512,512]{1,2,0:T(8,128)(2,1)}, u32[]{:S(2)}, u32[]{:S(2)}) async-start(bf16[16,512,512]{1,2,0:T(8,128)(2,1)} %stack.2), calls=%async_computation | async-start | bytes 16777216 | tf_op jit(solution)/shard_map/all_to_all | solution.py:14
Sparse Core Ops, SparseCore 0:
  9.0 34.5 all-gather.2
  46.3 68.3 all-reduce.4
  157.9 163.5 all-gather.4
